TPU v7x, 512 devices: a whole 4x8x8 slice. The times are simulated.
512 devices in a mesh: dp: 4 (over x_hi, core), context: 16 (over x_lo, z), tensor: 8 (over y).
Axes of the slice: x: 4 (x_hi: 2, x_lo: 2; x = x_hi * 2 + x_lo), y: 8, z: 8, core: 2. Of those that a mesh axis runs over, the one named last changes fastest.
Arguments:
- tokens: bfloat16 [32768, 4096], P(('dp', 'context', 'tensor')), parts along dimension 0, may hold values from -6 to 6
- norm_gain: bfloat16 [4096], replicated, may hold values from 0.099609375 to 1.8984375
- w_query: bfloat16 [4096, 2048], P(None, 'tensor'), may hold values from -2.03125 to 2.03125
- key_matrix: bfloat16 [4096, 1024], P(None, 'tensor'), may hold values from -0.109375 to 0.109375
- value_matrix: bfloat16 [4096, 1024], P(None, 'tensor'), may hold values from -0.09375 to 0.09375
- seg_ids: int32 [32768], P('dp'), parts along dimension 0, may hold values from 0 to 7, never falling along the last dimension, each value on 1 to 4096 neighbouring positions
Outputs:
- attended: bfloat16 [32768, 2048], P(('dp', 'context'), 'tensor'), parts along dimension 0
There are 4 independent parts, one for each index of `dp`. A program takes and returns all parts, laid end to end along the dimension named above; an argument that names none is the same for every part. Nothing has to cross between parts.
Inputs may be any that keep to these rules, and one draw needn't show every extreme that they name: `seg_ids`: never falls along the row; each of the 8 documents covers 1 to 4096 positions, one exactly 4096.
All inputs are finite; a program needn't handle non-finite values.
Results may differ from a plain program's by a relative error of at most 0.0078.
Values may be sent and summed in bfloat16 or wider, within the bound.
A program may use at most 64 MiB of HBM per device.

v0:
```python
import math
import jax
import jax.numpy as jnp
from jax import lax
from jax.sharding import PartitionSpec as P

HEAD_SIZE = 128


def sent_together(arrays, axis, dim, along):
    widths = [a.shape[along] for a in arrays]
    both = jnp.concatenate(arrays, axis=along)
    filled = lax.all_gather(both, axis, axis=dim, tiled=True)
    return tuple(jnp.split(filled, [sum(widths[:k]) for k in range(1, len(widths))], axis=along))


def rotate(vectors, positions):
    half_width = vectors.shape[-1] // 2
    inv_freq = jnp.exp(
        -(jnp.arange(half_width, dtype=jnp.float32) * (2.0 / vectors.shape[-1]))
        * math.log(500000.0)
    )
    angles = positions.astype(jnp.float32)[:, None] * inv_freq[None, :]
    cosine = jnp.cos(angles)[:, None, :]
    sine = jnp.sin(angles)[:, None, :]
    front_half = vectors[..., :half_width]
    back_half = vectors[..., half_width:]
    return jnp.concatenate(
        [front_half * cosine - back_half * sine, back_half * cosine + front_half * sine], -1
    )


def merge_block(
    states_in, query_heads, query_pos, query_segs, key_part, val_part, key_segs, key_pos
):
    peak_old, totals, weighted = states_in
    scores = jnp.einsum(
        "qkgd,skd->kgqs", query_heads, key_part, preferred_element_type=jnp.float32
    ) * (1.0 / math.sqrt(HEAD_SIZE))
    visible = (key_pos[None, :] <= query_pos[:, None]) & (key_segs[None, :] == query_segs[:, None])
    scores = jnp.where(visible[None, None], scores, -1e30)
    peak_new = jnp.maximum(peak_old, jnp.max(scores, -1))
    probs = jnp.where(visible[None, None], jnp.exp(scores - peak_new[..., None]), 0.0)
    rescale = jnp.exp(peak_old - peak_new)
    totals = totals * rescale + jnp.sum(probs, -1)
    weighted = weighted * rescale[..., None] + jnp.einsum(
        "kgqs,skd->kgqd", probs.astype(jnp.bfloat16), val_part, preferred_element_type=jnp.float32
    )
    return (peak_new, totals, weighted)


def body(tokens, norm_gain, w_query, key_matrix, value_matrix, seg_ids):
    wide_tokens = tokens.astype(jnp.float32)
    rms_normalized = (
        wide_tokens
        * lax.rsqrt(jnp.mean(wide_tokens * wide_tokens, -1, keepdims=True) + 1e-05)
        * norm_gain.astype(jnp.float32)
    ).astype(jnp.bfloat16)
    pieces = lax.all_gather(rms_normalized, "tensor", axis=0, tiled=True)
    projected = jnp.concatenate(
        [
            jnp.dot(pieces, w_query, preferred_element_type=jnp.float32),
            jnp.dot(pieces, key_matrix, preferred_element_type=jnp.float32),
            jnp.dot(pieces, value_matrix, preferred_element_type=jnp.float32),
        ],
        1,
    )
    span_rows = projected.shape[0]
    width_q = w_query.shape[1]
    width_k = key_matrix.shape[1]
    heads_q = width_q // HEAD_SIZE
    heads_kv = width_k // HEAD_SIZE
    heads_per_group = heads_q // heads_kv
    offset = lax.axis_index("context") * span_rows
    positions = offset + jnp.arange(span_rows, dtype=jnp.int32)
    query = rotate(projected[:, :width_q].reshape(span_rows, heads_q, HEAD_SIZE), positions).astype(
        jnp.bfloat16
    )
    key = rotate(
        projected[:, width_q : width_q + width_k].reshape(span_rows, heads_kv, HEAD_SIZE), positions
    ).astype(jnp.bfloat16)
    key = key.reshape(span_rows, width_k)
    value_rows = projected[:, width_q + width_k :].astype(jnp.bfloat16)
    groups = (query, positions, lax.dynamic_slice_in_dim(seg_ids, offset, span_rows, 0))
    query_rows, query_pos, query_segs = groups
    count = query_rows.shape[0]
    prepared = [
        (query_rows.reshape(count, heads_kv, heads_per_group, HEAD_SIZE), query_pos, query_segs)
    ]
    initial = [
        (
            jnp.full((heads_kv, heads_per_group, count), -1e30, jnp.float32),
            jnp.zeros((heads_kv, heads_per_group, count), jnp.float32),
            jnp.zeros((heads_kv, heads_per_group, count, HEAD_SIZE), jnp.float32),
        )
    ]
    states = tuple(initial)
    anchor = jnp.int32(0)
    keys_in, values_in = sent_together((key, value_rows), "context", 0, 1)
    length = keys_in.shape[0]
    sub_rows = math.gcd(length, 512)
    parts_count = length // sub_rows
    key_blocks = keys_in.reshape(parts_count, sub_rows, heads_kv, HEAD_SIZE)
    value_blocks = values_in.reshape(parts_count, sub_rows, heads_kv, HEAD_SIZE)
    key_pos_all = jnp.arange(length, dtype=jnp.int32)
    seg_blocks = seg_ids.reshape(parts_count, sub_rows)
    pos_blocks = key_pos_all.reshape(parts_count, sub_rows)
    results = []
    for (query_heads, query_pos, query_segs), states_in in zip(prepared, states):
        skipped = (anchor > jnp.max(query_pos)) | (seg_ids[length - 1] < jnp.min(query_segs))

        def update(carried, query_heads=query_heads, query_pos=query_pos, query_segs=query_segs):

            def inner(running, slices):
                key_part, val_part, key_segs, key_pos = slices
                return (
                    merge_block(
                        running,
                        query_heads,
                        query_pos,
                        query_segs,
                        key_part,
                        val_part,
                        key_segs,
                        key_pos,
                    ),
                    None,
                )

            return lax.scan(inner, carried, (key_blocks, value_blocks, seg_blocks, pos_blocks))[0]

        results.append(lax.cond(skipped, lambda carried: carried, update, states_in))
    finals = tuple(results)
    outputs = []
    for peak_val, totals, weighted in finals:
        count = weighted.shape[2]
        normalized = weighted / totals[..., None]
        outputs.append(
            jnp.transpose(normalized, (2, 0, 1, 3)).reshape(count, width_q).astype(jnp.bfloat16)
        )
    return outputs[0]


def solution(mesh):
    in_specs = (
        P(("dp", "context", "tensor"), None),
        P(),
        P(None, "tensor"),
        P(None, "tensor"),
        P(None, "tensor"),
        P("dp"),
    )
    out_specs = P(("dp", "context"), "tensor")
    return jax.shard_map(body, mesh=mesh, in_specs=in_specs, out_specs=out_specs, check_vma=False)
```

profile of v0, /device:TPU:8, one launch (start us, length us, event | category | flops | bytes accessed | tf_op | source)
XLA Modules:
  0.0 281.3 jit_solution(2508843274565658553)
XLA Ops:
  10.8 60.4 %all-gather.3.cloned.1.call-done = bf16[512,4096]{1,0:T(8,128)(2,1)} async-done(((bf16[64,4096]{1,0:T(8,128)(2,1)}), bf16[512,4096]{1,0:T(8,128)(2,1)}) %all-gather.3.cloned.1.call-update) | async-done | bytes 4194320 | tf_op jit(solution)/shard_map/all_gather | solution.py:59
  71.2 4.1 %convolution_bitcast_fusion.1 = f32[512,1,128]{0,2,1:T(8,128)S(1)} fusion(bf16[512,4096]{1,0:T(8,128)(2,1)} %all-gather.3.cloned.1.call-done, bf16[4096,128]{1,0:T(8,128)(2,1)} %param.13), kind=kOutput, calls=%fused_computation.37 | convolution fusion | flops 536870912 | bytes 5505024 | tf_op jit(solution)/shard_map/dot_general | solution.py:63
  84.1 3.5 %fusion.44 = f32[512,256]{0,1:T(8,128)S(1)} fusion(bf16[512,4096]{1,0:T(8,128)(2,1)} %all-gather.3.cloned.1.call-done, bf16[4096,256]{1,0:T(8,128)(2,1)S(1)} %copy-done), kind=kOutput, calls=%fused_computation.73 | convolution fusion | flops 1073741824 | bytes 6815744 | tf_op jit(solution)/shard_map/dot_general | solution.py:62
  89.4 69.8 %all-gather.5.cloned.1.call-done = bf16[8192,256]{0,1:T(8,128)(2,1)} async-done(((bf16[512,256]{0,1:T(8,128)(2,1)}), bf16[8192,256]{0,1:T(8,128)(2,1)}) %all-gather.5.cloned.1.call-update) | async-done | bytes 4194320 | tf_op jit(solution)/shard_map/all_gather | solution.py:13
  159.2 114.0 %conditional.1 = (f32[1,2,512]{2,1,0:T(2,128)S(1)}, f32[1,2,512,128]{3,2,1,0:T(8,128)S(1)}) conditional(s32[]{:T(128)} %convert_element_type.47, (bf16[8192,256]{0,1:T(8,128)(2,1)}, s32[8192]{0:T(1024)S(1)}, s32[16,512]{1,0:T(8,128)S(1)}, s32[16,512]{1,0:T(8,128)S(1)}, s32[512]{0:T(512)S(1)}, /*index=5*/s32[512]{0:T(512)S(1)}, ...), branch_computations={%region_3.8_spmd, %region_8.9_spmd} | conditional | flops 276453376 | bytes 34325800 | solution.py:132
  159.2 6.4 %copy.10 = bf16[8192,256]{1,0:T(8,128)(2,1)} copy(bf16[8192,256]{0,1:T(8,128)(2,1)} %get-tuple-element.134) | data formatting | bytes 8388608 | tf_op jit(solution)/shard_map
  165.6 4.5 %fusion.42 = (bf16[8192,128]{1,0:T(8,128)(2,1)}, bf16[8192,128]{1,0:T(8,128)(2,1)}) fusion(bf16[8192,256]{1,0:T(8,128)(2,1)} %copy.10), kind=kLoop, calls=%fused_computation.71 | loop fusion | bytes 8388608 | tf_op jit(solution)/shard_map/split | solution.py:14
  170.1 103.1 %while.14 = (s32[]{:T(128)}, f32[1,2,512]{2,1,0:T(2,128)S(1)}, f32[1,2,512]{2,1,0:T(2,128)S(1)}, f32[1,2,512,128]{3,2,1,0:T(8,128)S(1)}, s32[16,512]{1,0:T(8,128...) while((s32[]{:T(128)}, f32[1,2,512]{2,1,0:T(2,128)S(1)}, ...), condition=%wide.region_7.7_spmd.clone, body=%wide.region_4.6_spmd.clone.sunk | while | flops 276436992 | bytes 17384616 | solution.py:130
  170.4 2.8 fusion.59
  176.9 2.8 fusion.59
  179.7 2.7 fusion.62
  183.3 2.8 fusion.59
  186.1 2.7 fusion.62
  189.8 2.8 fusion.59
  196.2 2.8 fusion.59
  202.6 2.8 fusion.59
  205.4 2.7 fusion.62
  209.1 2.8 fusion.59
  211.9 2.7 fusion.62
  215.5 2.8 fusion.59
  222.0 2.8 fusion.59
  228.4 2.8 fusion.59
  231.2 2.7 fusion.62
  234.9 2.8 fusion.59
  237.7 2.7 fusion.62
  241.3 2.8 fusion.59
  247.7 2.8 fusion.59
  250.5 2.7 fusion.62
  254.2 2.8 fusion.59
  257.0 2.7 fusion.62
  260.6 2.8 fusion.59
  267.1 2.8 fusion.59
  (177 shorter events, 50.0 us)
Async XLA Ops:
  6.5 77.6 %copy-start = (bf16[4096,256]{1,0:T(8,128)(2,1)S(1)}, bf16[4096,256]{1,0:T(8,128)(2,1)}, u32[]{:S(2)}) copy-start(bf16[4096,256]{1,0:T(8,128)(2,1)} %param.12) | copy-start | bytes 6291460
  6.5 64.7 %all-gather.3.cloned.1.call-start = ((), (), s32[]{:S(2)}) async-start(), calls=%async_computation | async-start | bytes 4718592 | tf_op jit(solution)/shard_map/all_gather | solution.py:59
  10.7 148.5 %all-gather.5.cloned.1.call-start = ((), (), s32[]{:S(2)}) async-start(), calls=%async_computation.1 | async-start | bytes 4456448 | tf_op jit(solution)/shard_map/all_gather | solution.py:13
  10.8 65.1 %copy-start.3 = (bf16[4096,128]{1,0:T(8,128)(2,1)S(1)}, bf16[4096,128]{1,0:T(8,128)(2,1)}, u32[]{:S(2)}) copy-start(bf16[4096,128]{1,0:T(8,128)(2,1)} %param.14) | copy-start | bytes 3145732
  71.2 4.7 %copy-start.2 = (bf16[512,4096]{1,0:T(8,128)(2,1)S(1)}, bf16[512,4096]{1,0:T(8,128)(2,1)}, u32[]{:S(2)}) copy-start(bf16[512,4096]{1,0:T(8,128)(2,1)} %all-gather.3.cloned.1.call-done) | copy-start | bytes 12582916
  75.9 3.0 %copy-start.4 = (s32[8192]{0:T(1024)S(1)}, s32[8192]{0:T(1024)}, u32[]{:S(2)}) copy-start(s32[8192]{0:T(1024)} %param.15) | copy-start | bytes 98308
  173.2 2.7 copy-start.1
  179.7 2.7 copy-start.1
  186.1 2.7 copy-start.1
  192.6 2.7 copy-start.1
  199.0 2.7 copy-start.1
  205.4 2.7 copy-start.1
  211.9 2.7 copy-start.1
  218.3 2.7 copy-start.1
  224.8 2.7 copy-start.1
  231.2 2.7 copy-start.1
  237.6 2.7 copy-start.1
  244.1 2.7 copy-start.1
  250.5 2.7 copy-start.1
  257.0 2.7 copy-start.1
  263.4 2.7 copy-start.1
  269.9 2.7 copy-start.1
Sparse Core Ops, SparseCore 0:
  10.8 60.3 all-gather.2
  78.3 80.8 all-gather.4
where the time goes:
time: 282 us; the launch traced here: 281 us
  waiting for transfers between devices  130 us (46%)
  matrix products  96.7 us (34%)
  other arithmetic  24.4 us (9%)
  between operations  15.6 us (6%)
  local copies, waits for them, and re-layouts  13.3 us (5%)
    all_gather x1, waiting for transfers between devices, sent_together(): filled = lax.all_gather(both, axis, axis=dim, tiled=True)  69.8 us
    all_gather x1, waiting for transfers between devices, body(): pieces = lax.all_gather(rms_normalized, 'tensor', axis=0, tiled=True)  60.4 us
    dot_general x16, matrix products, merge_block(): jnp.einsum('qkgd,skd->kgqs', query_heads, key_part, preferred_element_typ...  44.4 us
    dot_general x16, matrix products, merge_block(): jnp.einsum('kgqs,skd->kgqd', probs.astype(jnp.bfloat16), val_part, prefer...  43.2 us
    reduce_sum x16, other arithmetic, merge_block(): totals = totals * rescale + jnp.sum(probs, -1)  9.2 us
    another operation x1, local copies, waits for them, and re-layouts  6.43 us
  transfers between devices with their start and end apart: 2, of which 2 were waited for; matrix products, arithmetic and copies ran while one was open for 3% of the time, Pallas kernels for 0%

commit v1 on v0

--- a/solution.py
+++ b/solution.py
@@ -1,3 +1,4 @@
+import functools
 import math
 import jax
 import jax.numpy as jnp
@@ -5,6 +6,21 @@
 from jax.sharding import PartitionSpec as P
 
 HEAD_SIZE = 128
+
+
+def handle_the_pages(state, device_axis):
+    column = []
+    for _ in range(jax.lax.axis_size(device_axis)):
+        column.append(state)
+    return jnp.concatenate(
+        jax.lax.all_to_all(
+            jnp.stack(column, 0), axis_name=device_axis, split_axis=0, concat_axis=0
+        ),
+        0,
+    )
+
+
+build_sides = functools.partial(handle_the_pages, device_axis="tensor")
 
 
 def sent_together(arrays, axis, dim, along):
@@ -56,7 +72,7 @@
         * lax.rsqrt(jnp.mean(wide_tokens * wide_tokens, -1, keepdims=True) + 1e-05)
         * norm_gain.astype(jnp.float32)
     ).astype(jnp.bfloat16)
-    pieces = lax.all_gather(rms_normalized, "tensor", axis=0, tiled=True)
+    pieces = build_sides(rms_normalized)
     projected = jnp.concatenate(
         [
             jnp.dot(pieces, w_query, preferred_element_type=jnp.float32),

time: 282 us -> 311 us (1.10)
  waiting for transfers between devices: 130 us -> 162 us
  matrix products: 96.7 us -> 81.5 us
  starting transfers between devices: 0.04 us -> 10.3 us
  local copies, waits for them, and re-layouts: 13.3 us -> 18.9 us
    all_to_all x0 -> x1, waiting for transfers between devices: none -> 92.1 us  [handle_the_pages(): jax.lax.all_to_all(jnp.stack(column, 0), axis_name=device_axis, split_axi...]
    all_gather x1 -> x0, waiting for transfers between devices: 60.4 us -> none  [body(): pieces = lax.all_gather(rms_normalized, 'tensor', axis=0, tiled=True)]
    dot_general x16, matrix products: 44.4 us -> 25.2 us  [merge_block(): jnp.einsum('qkgd,skd->kgqs', query_heads, key_part, preferred_element_typ...]
    all_to_all x0 -> x1, starting transfers between devices: none -> 10.3 us  [handle_the_pages(): jax.lax.all_to_all(jnp.stack(column, 0), axis_name=device_axis, split_axi...]
    another operation x1 -> x3, local copies, waits for them, and re-layouts: 6.43 us -> 9.74 us
where the time goes in v1:
time: 311 us; the launch traced here: 310 us
  waiting for transfers between devices  162 us (52%)
  matrix products  81.5 us (26%)
  other arithmetic  21.8 us (7%)
  local copies, waits for them, and re-layouts  18.9 us (6%)
  between operations  15.3 us (5%)
  starting transfers between devices  10.3 us (3%)
    all_to_all x1, waiting for transfers between devices, handle_the_pages(): jax.lax.all_to_all(jnp.stack(column, 0), axis_name=device_axis, split_axi...  92.1 us
    all_gather x1, waiting for transfers between devices, sent_together(): filled = lax.all_gather(both, axis, axis=dim, tiled=True)  69.5 us
    dot_general x16, matrix products, merge_block(): jnp.einsum('kgqs,skd->kgqd', probs.astype(jnp.bfloat16), val_part, prefer...  44.5 us
    dot_general x16, matrix products, merge_block(): jnp.einsum('qkgd,skd->kgqs', query_heads, key_part, preferred_element_typ...  25.2 us
    all_to_all x1, starting transfers between devices, handle_the_pages(): jax.lax.all_to_all(jnp.stack(column, 0), axis_name=device_axis, split_axi...  10.3 us
    reduce_sum x16, other arithmetic, merge_block(): totals = totals * rescale + jnp.sum(probs, -1)  9.06 us
    another operation x2, local copies, waits for them, and re-layouts  7.27 us
  transfers between devices with their start and end apart: 2, of which 2 were waited for; matrix products, arithmetic and copies ran while one was open for 3% of the time, Pallas kernels for 0%

profile of v1, /device:TPU:8, one launch (start us, length us, event | category | flops | bytes accessed | tf_op | source)
XLA Modules:
  0.0 310.3 jit_solution(12956365477695012744)
XLA Ops:
  9.8 2.5 stack.2
  12.3 10.3 %all-to-all-start = ((bf16[8,64,4096]{2,1,0:T(8,128)(2,1)}), bf16[8,64,4096]{2,1,0:T(8,128)(2,1)}, u32[]{:S(2)}, u32[]{:S(2)}) async-start(bf16[8,64,4096]{2,1,0:T(8,128)(2,1)} %stack.2), calls=%async_computation | async-start | bytes 8388608 | tf_op jit(solution)/shard_map/all_to_all | solution.py:16
  22.6 92.1 %all-to-all-done = bf16[8,64,4096]{2,1,0:T(8,128)(2,1)} async-done(((bf16[8,64,4096]{2,1,0:T(8,128)(2,1)}), bf16[8,64,4096]{2,1,0:T(8,128)(2,1)}, u32[]{:S(2)}, u32[]{:S(2)}) %all-to-all-start) | async-done | bytes 4194336 | tf_op jit(solution)/shard_map/all_to_all | solution.py:16
  114.6 3.8 %convolution_bitcast_fusion.1 = f32[512,1,128]{0,2,1:T(8,128)S(1)} fusion(bf16[512,4096]{1,0:T(8,128)(2,1)} %bitcast.3, bf16[4096,128]{1,0:T(8,128)(2,1)S(1)} %copy-done), kind=kOutput, calls=%fused_computation.37 | convolution fusion | flops 536870912 | bytes 5505024 | tf_op jit(solution)/shard_map/dot_general | solution.py:79
  118.4 3.8 %convolution_convert_fusion = bf16[512,128]{0,1:T(8,128)(2,1)S(1)} fusion(bf16[512,4096]{1,0:T(8,128)(2,1)} %bitcast.3, bf16[4096,128]{1,0:T(8,128)(2,1)S(1)} %copy-done.2), kind=kOutput, calls=%fused_computation.38 | convolution fusion | flops 536936448 | bytes 5373952 | tf_op jit(solution)/shard_map/dot_general | solution.py:80
  124.3 2.9 copy.13
  130.8 4.2 %fusion.43 = f32[512,2,128]{0,2,1:T(8,128)S(1)} fusion(bf16[512,4096,1]{1,0,2:T(8,128)(2,1)} %bitcast.7, bf16[2,128,4096]{2,1,0:T(8,128)(2,1)} %bitcast.110), kind=kOutput, calls=%fused_computation.72 | convolution fusion | flops 1073741824 | bytes 6815744 | tf_op jit(solution)/shard_map/dot_general | solution.py:78
  135.1 69.5 %all-gather.2.cloned.1.call-done = bf16[8192,256]{0,1:T(8,128)(2,1)} async-done(((bf16[512,256]{0,1:T(8,128)(2,1)}), bf16[8192,256]{0,1:T(8,128)(2,1)}) %all-gather.2.cloned.1.call-update) | async-done | bytes 4194320 | tf_op jit(solution)/shard_map/all_gather | solution.py:29
  204.6 96.6 %conditional.1 = (f32[1,2,512]{2,1,0:T(2,128)S(1)}, f32[1,2,512,128]{3,2,1,0:T(8,128)}) conditional(s32[]{:T(128)} %convert_element_type.47, (bf16[8192,256]{0,1:T(8,128)(2,1)}, s32[8192]{0:T(1024)S(1)}, s32[16,512]{1,0:T(8,128)S(1)}, s32[16,512]{1,0:T(8,128)S(1)}, s32[512]{0:T(512)S(1)}, /*index=5*/s32[512]{0:T(512)S(1)}, ...), branch_computations={%region_3.8_spmd, %region_8.9_spmd} | conditional | flops 276453376 | bytes 26461452 | solution.py:148
  204.6 6.4 %copy.9 = bf16[8192,256]{1,0:T(8,128)(2,1)} copy(bf16[8192,256]{0,1:T(8,128)(2,1)} %get-tuple-element.134) | data formatting | bytes 8388608 | tf_op jit(solution)/shard_map
  211.1 4.4 %fusion.42 = (bf16[8192,128]{1,0:T(8,128)(2,1)}, bf16[8192,128]{1,0:T(8,128)(2,1)}) fusion(bf16[8192,256]{1,0:T(8,128)(2,1)} %copy.9), kind=kLoop, calls=%fused_computation.71 | loop fusion | bytes 8388608 | tf_op jit(solution)/shard_map/split | solution.py:30
  216.4 84.8 %while.14 = (s32[]{:T(128)}, f32[1,2,512]{2,1,0:T(2,128)S(1)}, f32[1,2,512]{2,1,0:T(2,128)S(1)}, f32[1,2,512,128]{3,2,1,0:T(8,128)}, s32[16,512]{1,0:T(8,128)S(1...) while((s32[]{:T(128)}, f32[1,2,512]{2,1,0:T(2,128)S(1)}, ...), condition=%wide.region_7.7_spmd.clone, body=%wide.region_4.6_spmd.clone.sunk | while | flops 276436992 | bytes 8995981 | solution.py:146
  216.7 1.6 fusion.58
  218.3 2.6 fusion.61
  221.8 1.6 fusion.58
  223.4 2.8 fusion.61
  228.7 2.8 fusion.61
  232.4 1.6 fusion.58
  234.1 2.8 fusion.61
  239.4 2.8 fusion.61
  244.7 2.8 fusion.61
  250.0 2.8 fusion.61
  255.3 2.8 fusion.61
  259.0 1.6 fusion.58
  260.6 2.8 fusion.61
  265.9 2.8 fusion.61
  271.2 2.8 fusion.61
  276.6 2.8 fusion.61
  281.9 2.8 fusion.61
  287.2 2.8 fusion.61
  292.5 2.8 fusion.61
  297.8 2.8 fusion.61
  (143 shorter events, 43.4 us)
Async XLA Ops:
  6.5 108.1 %copy-start = (bf16[4096,128]{1,0:T(8,128)(2,1)S(1)}, bf16[4096,128]{1,0:T(8,128)(2,1)}, u32[]{:S(2)}) copy-start(bf16[4096,128]{1,0:T(8,128)(2,1)} %param.13) | copy-start | bytes 3145732
  12.3 102.3 %all-to-all-start = ((bf16[8,64,4096]{2,1,0:T(8,128)(2,1)}), bf16[8,64,4096]{2,1,0:T(8,128)(2,1)}, u32[]{:S(2)}, u32[]{:S(2)}) async-start(bf16[8,64,4096]{2,1,0:T(8,128)(2,1)} %stack.2), calls=%async_computation | async-start | bytes 8388608 | tf_op jit(solution)/shard_map/all_to_all | solution.py:16
  22.6 182.1 %all-gather.2.cloned.1.call-start = ((), (), s32[]{:S(2)}) async-start(), calls=%async_computation.1 | async-start | bytes 4456448 | tf_op jit(solution)/shard_map/all_gather | solution.py:29
  114.6 3.8 %copy-start.2 = (bf16[4096,128]{1,0:T(8,128)(2,1)S(1)}, bf16[4096,128]{1,0:T(8,128)(2,1)}, u32[]{:S(2)}) copy-start(bf16[4096,128]{1,0:T(8,128)(2,1)} %param.14) | copy-start | bytes 3145732
  118.4 5.8 %copy-start.1 = (bf16[4096,256]{1,0:T(8,128)(2,1)S(1)}, bf16[4096,256]{1,0:T(8,128)(2,1)}, u32[]{:S(2)}) copy-start(bf16[4096,256]{1,0:T(8,128)(2,1)} %param.12) | copy-start | bytes 6291460
  124.3 2.9 copy-start.3
Sparse Core Ops, SparseCore 0:
  123.7 80.8 all-gather.1
